TPU v7x, 32 devices: a whole 2x2x4 slice. The times are simulated.
32 devices in a mesh: dom: 16 (over z, y, x), band: 2 (over core).
Axes of the slice: x: 2, y: 2, z: 4, core: 2. Of those that a mesh axis runs over, the one named last changes fastest.
Arguments:
- vectors: bfloat16 [8192, 768], P('dom', 'band'), may hold values from -16 to 16
- cell_ham: bfloat16 [8, 512, 512], replicated, may hold values from -0.25 to 0.25
- cell_type: int32 [32], P('dom'), may hold values from 0 to 7
- cell_nodes: int32 [32, 512], P('dom'), may hold values from 0 to 767, as said below
- shared_nodes: int32 [16, 256], P('dom'), may hold values from 0 to 511, as said below
Outputs:
- filtered: bfloat16 [8192, 768], P('dom', 'band')
- margin: float32 [2, 384, 768], P('band', 'dom')
Inputs may be any that keep to these rules, and one draw needn't show every extreme that they name: `cell_nodes`: the 512 entries of each cell are distinct. `shared_nodes`: the 256 entries of each row are distinct.
All inputs are finite; a program needn't handle non-finite values.
Results may differ from a plain program's by a relative error of at most 0.0045.
Values may be sent and summed in bfloat16 or wider, within the bound.
A program may use at most 64 MiB of HBM per device.

v0:
```python
import jax
import jax.numpy as jnp
from jax import lax
from jax.sharding import PartitionSpec as P

SHIFT = 0.5
INV_HALF = 0.5


def extended_2(cells, sides, width):
    for axis, dim in sides:
        count = lax.axis_size(axis)
        ends = count - 1
        head = lax.slice_in_dim(cells, 0, width, axis=dim)
        tail = lax.slice_in_dim(cells, cells.shape[dim] - width, cells.shape[dim], axis=dim)
        cells = jnp.concatenate(
            [
                lax.ppermute(tail, axis, [(i, (i + 1) % count) for i in range(ends)]),
                cells,
                lax.ppermute(head, axis, [((i + 1) % count, i) for i in range(ends)]),
            ],
            axis=dim,
        )
    return cells


def apply_cells(extended, cell_ham, cell_type, cell_nodes):
    accumulated = jnp.zeros(extended.shape, jnp.float32)
    for number in range(cell_nodes.shape[0]):
        node_index = cell_nodes[number]
        cell_out = jnp.dot(
            cell_ham[cell_type[number]], extended[node_index], preferred_element_type=jnp.float32
        )
        accumulated = accumulated.at[node_index].add(cell_out)
    return accumulated


def extend(field, shared):
    rim_size = shared.shape[0] // 2
    border = extended_2(field[shared], (("dom", 0),), rim_size)
    return jnp.concatenate([border[:rim_size], field, border[-rim_size:]], axis=0)


def settle(partial_value, shared, received):
    rim_size = shared.shape[0] // 2
    owned_rows = partial_value[rim_size:-rim_size]
    return (
        owned_rows.at[shared[:rim_size]]
        .add(received[:rim_size])
        .at[shared[rim_size:]]
        .add(received[-rim_size:])
    )


def assemble(partial_value, shared):
    rim_size = shared.shape[0] // 2
    outgoing = jnp.concatenate([partial_value[:rim_size], partial_value[-rim_size:]], axis=0)
    received = extended_2(outgoing.astype(jnp.bfloat16), (("dom", 0),), rim_size).astype(
        outgoing.dtype
    )
    return settle(partial_value, shared, received)


def on_device(vectors, cell_ham, cell_type, cell_nodes, shared_nodes):
    shared = shared_nodes[0]
    rim_size = shared.shape[0] // 2
    node_count = vectors.shape[0]
    initial_f = vectors.astype(jnp.float32)
    widened = extend(vectors, shared)
    partial_value = apply_cells(widened, cell_ham, cell_type, cell_nodes)
    outgoing = jnp.concatenate([partial_value[:rim_size], partial_value[-rim_size:]], axis=0)
    received = extended_2(outgoing, (("dom", 0),), rim_size)
    summed = settle(partial_value, shared, received)
    first_section = ((summed - SHIFT * initial_f) * INV_HALF).astype(jnp.bfloat16)
    border = extended_2(first_section[shared], (("dom", 0),), rim_size)
    first_wide = jnp.concatenate([border[:rim_size], first_section, border[-rim_size:]], axis=0)
    second = apply_cells(first_wide, cell_ham, cell_type, cell_nodes)
    settled = assemble(second, shared)
    filtered = (
        2.0 * (settled - SHIFT * first_section.astype(jnp.float32)) * INV_HALF - initial_f
    ).astype(jnp.bfloat16)
    inverse_count = 1.0 / (node_count * lax.axis_size("dom"))
    everyone = lax.all_gather(filtered, "band", axis=1, tiled=True)
    result_rows = (
        lax.psum_scatter(
            lax.dot_general(
                filtered, everyone, (((0,), (0,)), ((), ())), preferred_element_type=jnp.float32
            ),
            "dom",
            scatter_dimension=0,
            tiled=True,
        )
        * inverse_count
    )
    return (filtered, result_rows[None])


def solution(mesh):
    in_specs = (P("dom", "band"), P(), P("dom"), P("dom", None), P("dom", None))
    out_specs = (P("dom", "band"), P("band", "dom", None))
    return jax.shard_map(
        on_device, mesh=mesh, in_specs=in_specs, out_specs=out_specs, check_vma=False
    )
```

profile of v0, /device:TPU:0, one launch (start us, length us, event | category | flops | bytes accessed | tf_op | source)
XLA Modules:
  0.0 234.1 jit_solution(16663798027381683443)
XLA Ops:
  7.9 2.3 gather_fusion
  10.2 1.3 collective-permute-start.1
  11.5 5.5 %collective-permute-start = (bf16[128,384]{1,0:T(8,128)(2,1)S(1)}, bf16[128,384]{1,0:T(8,128)(2,1)S(1)}, u32[]{:S(2)}, u32[]{:S(2)}) collective-permute-start(bf16[128,384]{1,0:T(8,128)(2,1)S(1)} %get-tuple-element.9), channel_id=1, source_target_pairs={{0,2},{2,4},{4,6},{6,8},{8,10},{10,12},{12,14},{14,16},{16,18},{18... | collective-permute-start | bytes 294920 | tf_op jit(solution)/shard_map/ppermute | solution.py:18
  21.7 1.9 gather_fusion.2
  23.6 1.9 gather_fusion.1
  25.6 1.5 fusion.14
  27.0 3.9 %scatter_custom_fusion = f32[768,384]{1,0:T(8,128)S(1)} fusion(s32[512]{0:T(512)S(1)} %bitcast.41, f32[512,384]{1,0:T(8,128)S(1)} %fusion.14, f32[]{:T(128)} %constant.7.clone.1), kind=kCustom, calls=%fused_computation.23 | custom fusion | flops 196608 | bytes 1179652 | tf_op jit(solution)/shard_map/scatter-add | solution.py:34
  30.9 1.5 fusion.10
  32.4 4.0 %scatter_fusion = f32[768,384]{1,0:T(8,128)S(1)} fusion(f32[768,384]{1,0:T(8,128)S(1)} %scatter_custom_fusion, s32[512]{0:T(512)S(1)} %bitcast.38, f32[512,384]{1,0:T(8,128)S(1)} %fusion.10), kind=kCustom, calls=%fused_computation.7 | custom fusion | flops 196608 | bytes 2361344 | tf_op jit(solution)/shard_map/scatter-add | solution.py:34
  36.5 1.3 collective-permute-start.3
  37.8 5.5 %collective-permute-start.2 = (f32[128,384]{1,0:T(8,128)S(1)}, f32[128,384]{1,0:T(8,128)S(1)}, u32[]{:S(2)}, u32[]{:S(2)}) collective-permute-start(f32[128,384]{1,0:T(8,128)S(1)} %get-tuple-element.3), channel_id=1, source_target_pairs={{0,2},{2,4},{4,6},{6,8},{8,10},{10,12},{12,14},{14,16},{16,18},{18... | collective-permute-start | bytes 589832 | tf_op jit(solution)/shard_map/ppermute | solution.py:18
  43.4 7.7 %collective-permute-done.2 = f32[128,384]{1,0:T(8,128)S(1)} collective-permute-done((f32[128,384]{1,0:T(8,128)S(1)}, f32[128,384]{1,0:T(8,128)S(1)}, u32[]{:S(2)}, u32[]{:S(2)}) %collective-permute-start.2) | collective-permute-done | bytes 196640 | tf_op jit(solution)/shard_map/ppermute | solution.py:18
  51.1 1.6 scatter_fusion.1
  52.7 1.7 scatter_fusion.2
  55.7 4.4 %collective-permute-start.4 = (bf16[128,384]{1,0:T(8,128)(2,1)S(1)}, bf16[128,384]{1,0:T(8,128)(2,1)S(1)}, u32[]{:S(2)}, u32[]{:S(2)}) collective-permute-start(bf16[128,384]{1,0:T(8,128)(2,1)S(1)} %get-tuple-element.6), channel_id=1, source_target_pairs={{0,2},{2,4},{4,6},{6,8},{8,10},{10,12},{12,14},{14,16},{16,18},{18... | collective-permute-start | bytes 294920 | tf_op jit(solution)/shard_map/ppermute | solution.py:18
  60.1 1.5 collective-permute-start.5
  62.3 4.3 %collective-permute-done.5 = bf16[128,384]{1,0:T(8,128)(2,1)S(1)} collective-permute-done((bf16[128,384]{1,0:T(8,128)(2,1)S(1)}, bf16[128,384]{1,0:T(8,128)(2,1)S(1)}, u32[]{:S(2)}, u32[]{:S(2)}) %collective-permute-start.5) | collective-permute-done | bytes 98336 | tf_op jit(solution)/shard_map/ppermute | solution.py:20
  66.7 1.9 gather_fusion.5
  68.6 1.9 gather_fusion.4
  70.6 1.5 fusion.12
  72.0 3.9 %scatter_custom_fusion.4 = f32[768,384]{1,0:T(8,128)S(1)} fusion(s32[512]{0:T(512)S(1)} %bitcast.42, f32[512,384]{1,0:T(8,128)S(1)} %fusion.12, f32[]{:T(128)} %constant.7.clone.1), kind=kCustom, calls=%fused_computation.21 | custom fusion | flops 196608 | bytes 1179652 | tf_op jit(solution)/shard_map/scatter-add | solution.py:34
  75.9 1.5 fusion.8
  77.4 4.0 %scatter_fusion.3 = f32[768,384]{1,0:T(8,128)S(1)} fusion(f32[768,384]{1,0:T(8,128)S(1)} %scatter_custom_fusion.4, s32[512]{0:T(512)S(1)} %bitcast.39, f32[512,384]{1,0:T(8,128)S(1)} %fusion.8), kind=kCustom, calls=%fused_computation.11 | custom fusion | flops 196608 | bytes 2361344 | tf_op jit(solution)/shard_map/scatter-add | solution.py:34
  81.6 2.8 %collective-permute-start.6 = (bf16[128,384]{1,0:T(8,128)(2,1)S(1)}, bf16[128,384]{1,0:T(8,128)(2,1)S(1)}, u32[]{:S(2)}, u32[]{:S(2)}) collective-permute-start(bf16[128,384]{1,0:T(8,128)(2,1)S(1)} %get-tuple-element.4), channel_id=1, source_target_pairs={{0,2},{2,4},{4,6},{6,8},{8,10},{10,12},{12,14},{14,16},{16,18},{18... | collective-permute-start | bytes 294920 | tf_op jit(solution)/shard_map/ppermute | solution.py:18
  84.4 1.3 collective-permute-start.7
  86.6 4.4 %collective-permute-done.7 = bf16[128,384]{1,0:T(8,128)(2,1)S(1)} collective-permute-done((bf16[128,384]{1,0:T(8,128)(2,1)S(1)}, bf16[128,384]{1,0:T(8,128)(2,1)S(1)}, u32[]{:S(2)}, u32[]{:S(2)}) %collective-permute-start.7) | collective-permute-done | bytes 98336 | tf_op jit(solution)/shard_map/ppermute | solution.py:20
  91.0 1.7 scatter_custom_fusion.6
  92.6 1.7 scatter_custom_fusion.7
  94.5 2.4 %all_gather.3 = bf16[512,768]{1,0:T(8,128)(2,1)S(1)} all-gather(bf16[512,384]{1,0:T(8,128)(2,1)S(1)} %fusion.3), channel_id=1, replica_groups=mesh['dom'=16,'band'=2] {'band'}, dimensions={1}, use_global_device_ids=true | all-gather | bytes 1179648 | tf_op jit(solution)/shard_map/all_gather | solution.py:83
  96.8 1.5 fusion.43
  98.4 127.4 %reduce-scatter.2.cloned.1.call-done = f32[24,768]{1,0:T(8,128)} async-done(((f32[384,768]{1,0:T(8,128)}), f32[24,768]{1,0:T(8,128)}) %reduce-scatter.2.cloned.1.call-update) | async-done | bytes 73744 | tf_op jit(solution)/shard_map/reduce_scatter | solution.py:85
  225.7 1.5 multiply_bitcast_fusion
  (37 shorter events, 4.8 us)
Async XLA Ops:
  7.2 9.8 %copy-start.4 = (s32[2]{0:T(128)S(1)}, s32[2]{0:T(128)}, u32[]{:S(2)}) copy-start(s32[2]{0:T(128)} %param.7) | copy-start | bytes 28
  7.2 13.0 %copy-start.2 = (s32[2,512]{1,0:T(2,128)S(1)}, s32[2,512]{1,0:T(2,128)}, u32[]{:S(2)}) copy-start(s32[2,512]{1,0:T(2,128)} %param.8) | copy-start | bytes 12292
  7.2 218.6 %reduce-scatter.2.cloned.1.call-start = ((), (), s32[]{:S(2)}) async-start(), calls=%async_computation.1 | async-start | bytes 1253376 | tf_op jit(solution)/shard_map/reduce_scatter | solution.py:85
  7.9 13.6 %copy-start = (bf16[512,384]{1,0:T(8,128)(2,1)S(1)}, bf16[512,384]{1,0:T(8,128)(2,1)}, u32[]{:S(2)}) copy-start(bf16[512,384]{1,0:T(8,128)(2,1)} %param.5) | copy-start | bytes 1179652
  10.2 11.4 %collective-permute-start.1 = (bf16[128,384]{1,0:T(8,128)(2,1)S(1)}, bf16[128,384]{1,0:T(8,128)(2,1)S(1)}, u32[]{:S(2)}, u32[]{:S(2)}) collective-permute-start(bf16[128,384]{1,0:T(8,128)(2,1)S(1)} %get-tuple-element.8), channel_id=1, source_target_pairs={{2,0},{4,2},{6,4},{8,6},{10,8},{12,10},{14,12},{16,14},{18,16},{20... | collective-permute-start | bytes 294920 | tf_op jit(solution)/shard_map/ppermute | solution.py:20
  11.5 10.0 %collective-permute-start = (bf16[128,384]{1,0:T(8,128)(2,1)S(1)}, bf16[128,384]{1,0:T(8,128)(2,1)S(1)}, u32[]{:S(2)}, u32[]{:S(2)}) collective-permute-start(bf16[128,384]{1,0:T(8,128)(2,1)S(1)} %get-tuple-element.9), channel_id=1, source_target_pairs={{0,2},{2,4},{4,6},{6,8},{8,10},{10,12},{12,14},{14,16},{16,18},{18... | collective-permute-start | bytes 294920 | tf_op jit(solution)/shard_map/ppermute | solution.py:18
  32.4 10.9 %copy-start.3 = (s32[1,256]{1,0:T(1,128)S(1)}, s32[1,256]{1,0:T(1,128)}, u32[]{:S(2)}) copy-start(s32[1,256]{1,0:T(1,128)} %param.9) | copy-start | bytes 3076
  36.5 16.2 %collective-permute-start.3 = (f32[128,384]{1,0:T(8,128)S(1)}, f32[128,384]{1,0:T(8,128)S(1)}, u32[]{:S(2)}, u32[]{:S(2)}) collective-permute-start(f32[128,384]{1,0:T(8,128)S(1)} %get-tuple-element.2), channel_id=1, source_target_pairs={{2,0},{4,2},{6,4},{8,6},{10,8},{12,10},{14,12},{16,14},{18,16},{20... | collective-permute-start | bytes 589832 | tf_op jit(solution)/shard_map/ppermute | solution.py:20
  37.8 13.2 %collective-permute-start.2 = (f32[128,384]{1,0:T(8,128)S(1)}, f32[128,384]{1,0:T(8,128)S(1)}, u32[]{:S(2)}, u32[]{:S(2)}) collective-permute-start(f32[128,384]{1,0:T(8,128)S(1)} %get-tuple-element.3), channel_id=1, source_target_pairs={{0,2},{2,4},{4,6},{6,8},{8,10},{10,12},{12,14},{14,16},{16,18},{18... | collective-permute-start | bytes 589832 | tf_op jit(solution)/shard_map/ppermute | solution.py:18
  55.7 6.6 %collective-permute-start.4 = (bf16[128,384]{1,0:T(8,128)(2,1)S(1)}, bf16[128,384]{1,0:T(8,128)(2,1)S(1)}, u32[]{:S(2)}, u32[]{:S(2)}) collective-permute-start(bf16[128,384]{1,0:T(8,128)(2,1)S(1)} %get-tuple-element.6), channel_id=1, source_target_pairs={{0,2},{2,4},{4,6},{6,8},{8,10},{10,12},{12,14},{14,16},{16,18},{18... | collective-permute-start | bytes 294920 | tf_op jit(solution)/shard_map/ppermute | solution.py:18
  60.1 6.5 %collective-permute-start.5 = (bf16[128,384]{1,0:T(8,128)(2,1)S(1)}, bf16[128,384]{1,0:T(8,128)(2,1)S(1)}, u32[]{:S(2)}, u32[]{:S(2)}) collective-permute-start(bf16[128,384]{1,0:T(8,128)(2,1)S(1)} %get-tuple-element.7), channel_id=1, source_target_pairs={{2,0},{4,2},{6,4},{8,6},{10,8},{12,10},{14,12},{16,14},{18,16},{20... | collective-permute-start | bytes 294920 | tf_op jit(solution)/shard_map/ppermute | solution.py:20
  81.6 5.0 %collective-permute-start.6 = (bf16[128,384]{1,0:T(8,128)(2,1)S(1)}, bf16[128,384]{1,0:T(8,128)(2,1)S(1)}, u32[]{:S(2)}, u32[]{:S(2)}) collective-permute-start(bf16[128,384]{1,0:T(8,128)(2,1)S(1)} %get-tuple-element.4), channel_id=1, source_target_pairs={{0,2},{2,4},{4,6},{6,8},{8,10},{10,12},{12,14},{14,16},{16,18},{18... | collective-permute-start | bytes 294920 | tf_op jit(solution)/shard_map/ppermute | solution.py:18
  84.4 6.6 %collective-permute-start.7 = (bf16[128,384]{1,0:T(8,128)(2,1)S(1)}, bf16[128,384]{1,0:T(8,128)(2,1)S(1)}, u32[]{:S(2)}, u32[]{:S(2)}) collective-permute-start(bf16[128,384]{1,0:T(8,128)(2,1)S(1)} %get-tuple-element.5), channel_id=1, source_target_pairs={{2,0},{4,2},{6,4},{8,6},{10,8},{12,10},{14,12},{16,14},{18,16},{20... | collective-permute-start | bytes 294920 | tf_op jit(solution)/shard_map/ppermute | solution.py:20
  94.5 3.9 %copy-start.1 = (bf16[512,384]{1,0:T(8,128)(2,1)}, bf16[512,384]{1,0:T(8,128)(2,1)S(1)}, u32[]{:S(2)}) copy-start(bf16[512,384]{1,0:T(8,128)(2,1)S(1)} %fusion.3) | copy-start | bytes 1179652
Sparse Core Ops, SparseCore 0:
  98.5 127.1 reduce-scatter.1
where the time goes:
time: 235 us; the launch traced here: 234 us
  waiting for transfers between devices  145 us (62%)
  other arithmetic  25.1 us (11%)
  starting transfers between devices  23.5 us (10%)
  between operations  18.3 us (8%)
  local copies, waits for them, and re-layouts  12.1 us (5%)
  matrix products  7.43 us (3%)
  blocking collectives  2.37 us (1%)
    reduce_scatter x1, waiting for transfers between devices, on_device(): lax.psum_scatter(lax.dot_general(filtered, everyone, (((0,), (0,)), ((),...  127 us
    ppermute x4, starting transfers between devices, extended_2(): lax.ppermute(tail, axis, [(i, (i + 1) % count) for i in range(ends)])  18.1 us
    scatter-add x4, other arithmetic, apply_cells(): accumulated = accumulated.at[node_index].add(cell_out)  15.8 us
    ppermute x4, waiting for transfers between devices, extended_2(): lax.ppermute(tail, axis, [(i, (i + 1) % count) for i in range(ends)])  9.24 us
    ppermute x4, waiting for transfers between devices, extended_2(): lax.ppermute(head, axis, [((i + 1) % count, i) for i in range(ends)])  8.7 us
    gather x4, local copies, waits for them, and re-layouts, apply_cells(): extended[node_index]  7.75 us
    scatter-add x4, other arithmetic, settle(): return owned_rows.at[shared[:rim_size]].add(received[:rim_size]).at[share...  6.63 us
    dot_general x4, matrix products, apply_cells(): jnp.dot(cell_ham[cell_type[number]], extended[node_index], preferred_elem...  5.92 us
  transfers between devices with their start and end apart: 9, of which 6 were waited for; matrix products, arithmetic and copies ran while one was open for 1% of the time, Pallas kernels for 0%

commit v1 on v0

v1 whole, which is shorter than its diff:
```python
import functools

import jax
import jax.numpy as jnp
from jax import lax
from jax.experimental import pallas as pl
from jax.experimental.pallas import tpu as pltpu
from jax.sharding import PartitionSpec as P

SHIFT = 0.5
INV_HALF = 0.5
MESH = pl.DeviceIdType.MESH
F32 = jnp.float32
BF16 = jnp.bfloat16


def dot(a, b):
    return jnp.dot(a, b, preferred_element_type=F32)


def dot_tn(a, b):
    return lax.dot_general(a, b, (((0,), (0,)), ((), ())), preferred_element_type=F32)


def dot_nt(a, b):
    return lax.dot_general(a, b, (((1,), (1,)), ((), ())), preferred_element_type=F32)


def one_hot(rows, index_row):
    spots = lax.broadcasted_iota(jnp.int32, (rows, index_row.shape[1]), 0)
    return jnp.where(spots == index_row, 1.0, 0.0).astype(BF16)


def kernel(
    doms, bands, scatter_here, inverse_count,
    type_ref, nodes_ref, shared_ref, v_ref, ham_hbm,
    filt_ref, margin_ref,
    ham, hp, send1, ghost, send2, recv2, send3, recv3, everyone, part, own_part, arrived,
    ham_sem, s1, r1, s2, r2, s3, r3, s4, r4, s5, r5,
):
    dom = lax.axis_index("dom")
    band = lax.axis_index("band")
    nodes, cols = v_ref.shape
    cells, cell_size = nodes_ref.shape
    rim = shared_ref.shape[1] // 2
    slots = nodes + 2 * rim
    present = (dom > 0, dom < doms - 1)
    beside = (jnp.maximum(dom - 1, 0), jnp.minimum(dom + 1, doms - 1))

    load_ham = pltpu.make_async_copy(ham_hbm, ham, ham_sem)
    load_ham.start()

    barrier = pltpu.get_barrier_semaphore()
    for step in range(1, bands):
        pl.semaphore_signal(
            barrier, inc=1,
            device_id={"dom": dom, "band": lax.rem(band + step, bands)},
            device_id_type=MESH,
        )
    if scatter_here:
        for step in range(1, doms):
            pl.semaphore_signal(
                barrier, inc=1,
                device_id={"dom": lax.rem(dom + step, doms), "band": band},
                device_id_type=MESH,
            )
    else:
        for side in (0, 1):
            @pl.when(present[side])
            def _():
                pl.semaphore_signal(
                    barrier, inc=1,
                    device_id={"dom": beside[side], "band": band},
                    device_id_type=MESH,
                )

    for side in (0, 1):
        @pl.when(jnp.logical_not(present[side]))
        def _():
            ghost[side] = jnp.zeros((rim, cols), BF16)
            recv2[side] = jnp.zeros((2, rim, cols), BF16)
            recv3[side] = jnp.zeros((rim, cols), BF16)

    def swap(source, target, sent, got, side, arriving):
        return pltpu.make_async_remote_copy(
            src_ref=source.at[side],
            dst_ref=target.at[side if arriving else 1 - side],
            send_sem=sent.at[side],
            recv_sem=got.at[side if arriving else 1 - side],
            device_id={"dom": beside[side], "band": band},
            device_id_type=MESH,
        )

    def swap_start(*buffers):
        for side in (0, 1):
            @pl.when(present[side])
            def _():
                swap(*buffers, side, False).start()

    def swap_wait(*buffers):
        for side in (0, 1):
            @pl.when(present[side])
            def _():
                swap(*buffers, side, True).wait()

    v = v_ref[...]
    pick = one_hot(nodes, shared_ref[...])
    send1[...] = dot_tn(pick, v).astype(BF16).reshape(2, rim, cols)

    if scatter_here:
        pl.semaphore_wait(barrier, doms - 1 + bands - 1)
    else:
        if bands > 1:
            pl.semaphore_wait(barrier, bands - 1)
        for side in (0, 1):
            @pl.when(present[side])
            def _():
                pl.semaphore_wait(barrier, 1)
    swap_start(send1, ghost, s1, r1)

    load_ham.wait()
    for cell in range(cells):
        slot = nodes_ref[cell : cell + 1, :]
        slot = jnp.where(slot < rim, slot + nodes, jnp.where(slot < nodes + rim, slot - rim, slot))
        spread = one_hot(slots, slot)
        spread_ham = dot(spread, ham[type_ref[cell]]).astype(BF16)
        hp[cell] = dot_nt(spread_ham, spread).astype(BF16)

    def apply(low, high, own, rims):
        total = dot(hp[0, low:high, :nodes], own) + dot(hp[0, low:high, nodes:], rims)
        for cell in range(1, cells):
            total += dot(hp[cell, low:high, :nodes], own) + dot(hp[cell, low:high, nodes:], rims)
        return total

    swap_wait(send1, ghost, s1, r1)
    rims = ghost[...].reshape(2 * rim, cols)
    y_own = apply(0, nodes, v, rims)
    y_rim = apply(nodes, slots, v, rims)
    send2[:, 0] = y_rim.astype(BF16).reshape(2, rim, cols)
    send2[:, 1] = dot_tn(pick, y_own.astype(BF16)).astype(BF16).reshape(2, rim, cols)
    swap_start(send2, recv2, s2, r2)
    v32 = v.astype(F32)
    swap_wait(send2, recv2, s2, r2)
    y_own = y_own + dot(pick, recv2[:, 0].reshape(2 * rim, cols))
    y_rim = y_rim + recv2[:, 1].reshape(2 * rim, cols).astype(F32)
    first = ((y_own - SHIFT * v32) * INV_HALF).astype(BF16)
    first_rim = ((y_rim - SHIFT * rims.astype(F32)) * INV_HALF).reshape(2, rim, cols)
    first_rim = jnp.concatenate(
        [jnp.where(present[side], first_rim[side], 0.0) for side in (0, 1)], axis=0
    ).astype(BF16)

    send3[...] = apply(nodes, slots, first, first_rim).astype(BF16).reshape(2, rim, cols)
    swap_start(send3, recv3, s3, r3)
    second = apply(0, nodes, first, first_rim)
    swap_wait(send3, recv3, s3, r3)
    second = second + dot(pick, recv3[...].reshape(2 * rim, cols))
    filtered = (2.0 * (second - SHIFT * first.astype(F32)) * INV_HALF - v32).astype(BF16)
    filt_ref[...] = filtered

    def share(step):
        return pltpu.make_async_remote_copy(
            src_ref=filt_ref,
            dst_ref=everyone.at[bands - 1 - step],
            send_sem=s4.at[step],
            recv_sem=r4.at[bands - 1 - step],
            device_id={"dom": dom, "band": lax.rem(band + step, bands)},
            device_id_type=MESH,
        )

    for step in range(1, bands):
        share(step).start()

    def give(step, away):
        target = lax.rem(dom + away, doms)
        return pltpu.make_async_remote_copy(
            src_ref=part.at[step, target],
            dst_ref=arrived.at[step, doms - 1 - away],
            send_sem=s5.at[step, away],
            recv_sem=r5.at[step, doms - 1 - away],
            device_id={"dom": target, "band": band},
            device_id_type=MESH,
        )

    for step in range(bands):
        if step == 0:
            other = filtered
        else:
            taken = pltpu.make_async_remote_copy(
                src_ref=filt_ref, dst_ref=everyone.at[step - 1],
                send_sem=s4.at[step], recv_sem=r4.at[step - 1],
                device_id={"dom": dom, "band": lax.rem(band + step, bands)},
                device_id_type=MESH,
            )
            taken.wait_recv()
            other = everyone[step - 1]
        product = dot_tn(filtered, other)
        place = pl.ds(pl.multiple_of(lax.rem(band + step, bands) * cols, 128), cols)
        if scatter_here:
            product = product.reshape(doms, cols // doms, cols)
            part[step] = product.astype(BF16)
            own_part[step] = product
            for away in range(1, doms):
                give(step, away).start()
        else:
            margin_ref[0, :, place] = product

    if scatter_here:
        for step in range(bands):
            total = own_part[step, dom]
            for away in range(1, doms):
                pltpu.make_async_remote_copy(
                    src_ref=part.at[step, dom],
                    dst_ref=arrived.at[step, away - 1],
                    send_sem=s5.at[step, away],
                    recv_sem=r5.at[step, away - 1],
                    device_id={"dom": lax.rem(dom + away, doms), "band": band},
                    device_id_type=MESH,
                ).wait_recv()
                total += arrived[step, away - 1].astype(F32)
            place = pl.ds(pl.multiple_of(lax.rem(band + step, bands) * cols, 128), cols)
            margin_ref[0, :, place] = total * inverse_count
        for step in range(bands):
            for away in range(1, doms):
                give(step, away).wait_send()
    for step in range(1, bands):
        share(step).wait_send()


def solution(mesh):
    doms, bands = mesh.shape["dom"], mesh.shape["band"]

    def on_device(vectors, cell_ham, cell_type, cell_nodes, shared_nodes):
        nodes, cols = vectors.shape
        rim = shared_nodes.shape[1] // 2
        slots = nodes + 2 * rim
        rows = cols // doms
        scatter_here = cols % doms == 0 and rows % 8 == 0
        inverse_count = 1.0 / (nodes * doms)
        kept = (doms, rows) if scatter_here else (1, 8)
        filtered, margin = pl.pallas_call(
            functools.partial(kernel, doms, bands, scatter_here, inverse_count),
            out_shape=(
                jax.ShapeDtypeStruct((nodes, cols), BF16),
                jax.ShapeDtypeStruct((1, rows if scatter_here else cols, bands * cols), F32),
            ),
            in_specs=[pl.BlockSpec(memory_space=pltpu.SMEM)]
            + [pl.BlockSpec(memory_space=pltpu.VMEM)] * 3
            + [pl.BlockSpec(memory_space=pl.ANY)],
            out_specs=(pl.BlockSpec(memory_space=pltpu.VMEM),) * 2,
            scratch_shapes=[
                pltpu.VMEM(cell_ham.shape, BF16),
                pltpu.VMEM((cell_nodes.shape[0], slots, slots), BF16),
                pltpu.VMEM((2, rim, cols), BF16),
                pltpu.VMEM((2, rim, cols), BF16),
                pltpu.VMEM((2, 2, rim, cols), BF16),
                pltpu.VMEM((2, 2, rim, cols), BF16),
                pltpu.VMEM((2, rim, cols), BF16),
                pltpu.VMEM((2, rim, cols), BF16),
                pltpu.VMEM((max(bands - 1, 1), nodes, cols), BF16),
                pltpu.VMEM((bands, *kept, cols), BF16),
                pltpu.VMEM((bands, *kept, cols), F32),
                pltpu.VMEM((bands, *kept, cols), BF16),
                pltpu.SemaphoreType.DMA,
            ]
            + [pltpu.SemaphoreType.DMA((2,))] * 6
            + [pltpu.SemaphoreType.DMA((bands,))] * 2
            + [pltpu.SemaphoreType.DMA((bands, doms if scatter_here else 1))] * 2,
            compiler_params=pltpu.CompilerParams(
                collective_id=0, has_side_effects=True, vmem_limit_bytes=48 << 20
            ),
        )(cell_type, cell_nodes, shared_nodes, vectors, cell_ham)
        if not scatter_here:
            margin = inverse_count * lax.psum_scatter(
                margin, "dom", scatter_dimension=1, tiled=True
            )
        return filtered, margin

    in_specs = (P("dom", "band"), P(), P("dom"), P("dom", None), P("dom", None))
    out_specs = (P("dom", "band"), P("band", "dom", None))
    return jax.shard_map(
        on_device, mesh=mesh, in_specs=in_specs, out_specs=out_specs, check_vma=False
    )
```

time: 235 us -> 51.5 us (0.22)
  the two profiles are of different devices: /device:TPU:0 before, /device:TPU:24 now
where the time goes in v1:
time: 51.5 us; the launch traced here: 51.3 us
  Pallas kernels  44.1 us (86%)
  local copies, waits for them, and re-layouts  6.58 us (13%)
  between operations  0.65 us (1%)
    pallas_call x1, Pallas kernels, on_device(): pl.pallas_call(functools.partial(kernel, doms, bands, scatter_here, inver...  44.1 us
    unnamed x12, local copies, waits for them, and re-layouts  6.58 us

profile of v1, /device:TPU:24, one launch (start us, length us, event | category | flops | bytes accessed | tf_op | source)
XLA Modules:
  0.0 51.3 jit_solution(8237682054195373448)
XLA Ops:
  0.6 0.0 copy-start
  0.6 2.2 %copy-done = bf16[8,512,512]{2,1,0:T(8,128)(2,1)S(1)} copy-done((bf16[8,512,512]{2,1,0:T(8,128)(2,1)S(1)}, bf16[8,512,512]{2,1,0:T(8,128)(2,1)}, u32[]{:S(2)}) %copy-start) | copy-done | bytes 4194328
  2.8 0.0 copy-start.1
  2.8 1.0 %copy-done.1 = bf16[512,384]{1,0:T(8,128)(2,1)S(1)} copy-done((bf16[512,384]{1,0:T(8,128)(2,1)S(1)}, bf16[512,384]{1,0:T(8,128)(2,1)}, u32[]{:S(2)}) %copy-start.1) | copy-done | bytes 393240
  3.8 0.0 copy-start.2
  3.8 0.7 %copy-done.2 = s32[2,512]{1,0:T(2,128)S(1)} copy-done((s32[2,512]{1,0:T(2,128)S(1)}, s32[2,512]{1,0:T(2,128)}, u32[]{:S(2)}) %copy-start.2) | copy-done | bytes 4120
  4.5 0.0 copy-start.3
  4.5 0.7 %copy-done.3 = s32[1,256]{1,0:T(1,128)S(1)} copy-done((s32[1,256]{1,0:T(1,128)S(1)}, s32[1,256]{1,0:T(1,128)}, u32[]{:S(2)}) %copy-start.3) | copy-done | bytes 1048
  5.2 0.0 copy-start.4
  5.2 0.7 %copy-done.4 = s32[2]{0:T(128)S(1)} copy-done((s32[2]{0:T(128)S(1)}, s32[2]{0:T(128)}, u32[]{:S(2)}) %copy-start.4) | copy-done | bytes 32
  5.8 44.1 %shard_map.68 = (bf16[512,384]{1,0:T(8,128)(2,1)S(1)}, f32[1,24,768]{2,1,0:T(8,128)S(1)}) custom-call(s32[2]{0:T(128)S(1)} %copy-done.4, s32[2,512]{1,0:T(2,128)S(1)} %copy-done.2, s32[1,256]{1,0:T(1,128)S(1)} %copy-done.3, bf16[512,384]{1,0:T(8,128)(2,1)S(1)} %copy-done.1, bf16[8,512,512]{2,1,0:T(8,128)(2,1)S(1)} %copy-done), custom_call_target="tpu_custom_call" | custom-call | tf_op jit(solution)/shard_map/pallas_call | solution.py:240
  49.9 0.7 %copy.9 = bf16[512,384]{1,0:T(8,128)(2,1)} copy(bf16[512,384]{1,0:T(8,128)(2,1)S(1)} %get-tuple-element.4) | data formatting | bytes 786432
  50.7 0.6 %copy.10 = f32[1,24,768]{2,1,0:T(8,128)} copy(f32[1,24,768]{2,1,0:T(8,128)S(1)} %get-tuple-element.5) | data formatting | bytes 147456
Async XLA Ops:
  0.6 2.2 %copy-start = (bf16[8,512,512]{2,1,0:T(8,128)(2,1)S(1)}, bf16[8,512,512]{2,1,0:T(8,128)(2,1)}, u32[]{:S(2)}) copy-start(bf16[8,512,512]{2,1,0:T(8,128)(2,1)} %ham_hbm.1) | copy-start | bytes 12582916
  2.8 1.0 %copy-start.1 = (bf16[512,384]{1,0:T(8,128)(2,1)S(1)}, bf16[512,384]{1,0:T(8,128)(2,1)}, u32[]{:S(2)}) copy-start(bf16[512,384]{1,0:T(8,128)(2,1)} %v_ref.1) | copy-start | bytes 1179652
  3.8 0.7 %copy-start.2 = (s32[2,512]{1,0:T(2,128)S(1)}, s32[2,512]{1,0:T(2,128)}, u32[]{:S(2)}) copy-start(s32[2,512]{1,0:T(2,128)} %nodes_ref.1) | copy-start | bytes 12292
  4.5 0.7 %copy-start.3 = (s32[1,256]{1,0:T(1,128)S(1)}, s32[1,256]{1,0:T(1,128)}, u32[]{:S(2)}) copy-start(s32[1,256]{1,0:T(1,128)} %shared_ref.1) | copy-start | bytes 3076
  5.2 0.7 %copy-start.4 = (s32[2]{0:T(128)S(1)}, s32[2]{0:T(128)}, u32[]{:S(2)}) copy-start(s32[2]{0:T(128)} %type_ref.1) | copy-start | bytes 28

commit v2 on v1

--- a/solution.py
+++ b/solution.py
@@ -33,10 +33,10 @@
 
 def kernel(
     doms, bands, scatter_here, inverse_count,
-    type_ref, nodes_ref, shared_ref, v_ref, ham_hbm,
+    type_hbm, nodes_hbm, shared_hbm, v_hbm, ham_hbm,
     filt_ref, margin_ref,
-    ham, hp, send1, ghost, send2, recv2, send3, recv3, everyone, part, own_part, arrived,
-    ham_sem, s1, r1, s2, r2, s3, r3, s4, r4, s5, r5,
+    type_ref, nodes_ref, shared_ref, v_ref, ham, hp, send1, ghost, send2, recv2, send3, recv3, everyone, part, own_part, arrived,
+    in_sem, s1, r1, s2, r2, s3, r3, s4, r4, s5, r5,
 ):
     dom = lax.axis_index("dom")
     band = lax.axis_index("band")
@@ -47,8 +47,20 @@
     present = (dom > 0, dom < doms - 1)
     beside = (jnp.maximum(dom - 1, 0), jnp.minimum(dom + 1, doms - 1))
 
-    load_ham = pltpu.make_async_copy(ham_hbm, ham, ham_sem)
-    load_ham.start()
+    load_shared, load_v, load_nodes, load_type, load_ham = [
+        pltpu.make_async_copy(source, target, in_sem.at[number])
+        for number, (source, target) in enumerate(
+            (
+                (shared_hbm, shared_ref),
+                (v_hbm, v_ref),
+                (nodes_hbm, nodes_ref),
+                (type_hbm, type_ref),
+                (ham_hbm, ham),
+            )
+        )
+    ]
+    for load in (load_shared, load_v, load_nodes, load_type, load_ham):
+        load.start()
 
     barrier = pltpu.get_barrier_semaphore()
     for step in range(1, bands):
@@ -103,6 +115,8 @@
             def _():
                 swap(*buffers, side, True).wait()
 
+    load_shared.wait()
+    load_v.wait()
     v = v_ref[...]
     pick = one_hot(nodes, shared_ref[...])
     send1[...] = dot_tn(pick, v).astype(BF16).reshape(2, rim, cols)
@@ -118,6 +132,8 @@
                 pl.semaphore_wait(barrier, 1)
     swap_start(send1, ghost, s1, r1)
 
+    load_nodes.wait()
+    load_type.wait()
     load_ham.wait()
     for cell in range(cells):
         slot = nodes_ref[cell : cell + 1, :]
@@ -243,11 +259,13 @@
                 jax.ShapeDtypeStruct((nodes, cols), BF16),
                 jax.ShapeDtypeStruct((1, rows if scatter_here else cols, bands * cols), F32),
             ),
-            in_specs=[pl.BlockSpec(memory_space=pltpu.SMEM)]
-            + [pl.BlockSpec(memory_space=pltpu.VMEM)] * 3
-            + [pl.BlockSpec(memory_space=pl.ANY)],
+            in_specs=[pl.BlockSpec(memory_space=pltpu.HBM)] * 5,
             out_specs=(pl.BlockSpec(memory_space=pltpu.VMEM),) * 2,
             scratch_shapes=[
+                pltpu.SMEM(cell_type.shape, jnp.int32),
+                pltpu.VMEM(cell_nodes.shape, jnp.int32),
+                pltpu.VMEM(shared_nodes.shape, jnp.int32),
+                pltpu.VMEM(vectors.shape, BF16),
                 pltpu.VMEM(cell_ham.shape, BF16),
                 pltpu.VMEM((cell_nodes.shape[0], slots, slots), BF16),
                 pltpu.VMEM((2, rim, cols), BF16),
@@ -260,7 +278,7 @@
                 pltpu.VMEM((bands, *kept, cols), BF16),
                 pltpu.VMEM((bands, *kept, cols), F32),
                 pltpu.VMEM((bands, *kept, cols), BF16),
-                pltpu.SemaphoreType.DMA,
+                pltpu.SemaphoreType.DMA((5,)),
             ]
             + [pltpu.SemaphoreType.DMA((2,))] * 6
             + [pltpu.SemaphoreType.DMA((bands,))] * 2

time: 51.5 us -> 51.2 us (level)
  no operation moved by 1% of the time
where the time goes in v2:
time: 51.2 us; the launch traced here: 51 us
  Pallas kernels  43.7 us (85%)
  local copies, waits for them, and re-layouts  6.58 us (13%)
  between operations  0.65 us (1%)
    pallas_call x1, Pallas kernels, on_device(): pl.pallas_call(functools.partial(kernel, doms, bands, scatter_here, inver...  43.7 us
    unnamed x12, local copies, waits for them, and re-layouts  6.58 us

profile of v2, /device:TPU:24, one launch (start us, length us, event | category | flops | bytes accessed | tf_op | source)
XLA Modules:
  0.0 51.0 jit_solution(14911754324100241851)
XLA Ops:
  0.6 0.0 copy-start
  0.6 2.2 %copy-done = bf16[8,512,512]{2,1,0:T(8,128)(2,1)S(1)} copy-done((bf16[8,512,512]{2,1,0:T(8,128)(2,1)S(1)}, bf16[8,512,512]{2,1,0:T(8,128)(2,1)}, u32[]{:S(2)}) %copy-start) | copy-done | bytes 4194328
  2.8 0.0 copy-start.1
  2.8 1.0 %copy-done.1 = bf16[512,384]{1,0:T(8,128)(2,1)S(1)} copy-done((bf16[512,384]{1,0:T(8,128)(2,1)S(1)}, bf16[512,384]{1,0:T(8,128)(2,1)}, u32[]{:S(2)}) %copy-start.1) | copy-done | bytes 393240
  3.8 0.0 copy-start.2
  3.8 0.7 %copy-done.2 = s32[2,512]{1,0:T(2,128)S(1)} copy-done((s32[2,512]{1,0:T(2,128)S(1)}, s32[2,512]{1,0:T(2,128)}, u32[]{:S(2)}) %copy-start.2) | copy-done | bytes 4120
  4.5 0.0 copy-start.3
  4.5 0.7 %copy-done.3 = s32[1,256]{1,0:T(1,128)S(1)} copy-done((s32[1,256]{1,0:T(1,128)S(1)}, s32[1,256]{1,0:T(1,128)}, u32[]{:S(2)}) %copy-start.3) | copy-done | bytes 1048
  5.2 0.0 copy-start.4
  5.2 0.7 %copy-done.4 = s32[2]{0:T(128)S(1)} copy-done((s32[2]{0:T(128)S(1)}, s32[2]{0:T(128)}, u32[]{:S(2)}) %copy-start.4) | copy-done | bytes 32
  5.8 43.7 %shard_map.68 = (bf16[512,384]{1,0:T(8,128)(2,1)S(1)}, f32[1,24,768]{2,1,0:T(8,128)S(1)}) custom-call(s32[2]{0:T(128)S(1)} %copy-done.4, s32[2,512]{1,0:T(2,128)S(1)} %copy-done.2, s32[1,256]{1,0:T(1,128)S(1)} %copy-done.3, bf16[512,384]{1,0:T(8,128)(2,1)S(1)} %copy-done.1, bf16[8,512,512]{2,1,0:T(8,128)(2,1)S(1)} %copy-done), custom_call_target="tpu_custom_call" | custom-call | tf_op jit(solution)/shard_map/pallas_call | solution.py:256
  49.6 0.7 %copy.9 = bf16[512,384]{1,0:T(8,128)(2,1)} copy(bf16[512,384]{1,0:T(8,128)(2,1)S(1)} %get-tuple-element.4) | data formatting | bytes 786432
  50.3 0.6 %copy.10 = f32[1,24,768]{2,1,0:T(8,128)} copy(f32[1,24,768]{2,1,0:T(8,128)S(1)} %get-tuple-element.5) | data formatting | bytes 147456
Async XLA Ops:
  0.6 2.2 %copy-start = (bf16[8,512,512]{2,1,0:T(8,128)(2,1)S(1)}, bf16[8,512,512]{2,1,0:T(8,128)(2,1)}, u32[]{:S(2)}) copy-start(bf16[8,512,512]{2,1,0:T(8,128)(2,1)} %ham_hbm.1) | copy-start | bytes 12582916
  2.8 1.0 %copy-start.1 = (bf16[512,384]{1,0:T(8,128)(2,1)S(1)}, bf16[512,384]{1,0:T(8,128)(2,1)}, u32[]{:S(2)}) copy-start(bf16[512,384]{1,0:T(8,128)(2,1)} %v_hbm.1) | copy-start | bytes 1179652
  3.8 0.7 %copy-start.2 = (s32[2,512]{1,0:T(2,128)S(1)}, s32[2,512]{1,0:T(2,128)}, u32[]{:S(2)}) copy-start(s32[2,512]{1,0:T(2,128)} %nodes_hbm.1) | copy-start | bytes 12292
  4.5 0.7 %copy-start.3 = (s32[1,256]{1,0:T(1,128)S(1)}, s32[1,256]{1,0:T(1,128)}, u32[]{:S(2)}) copy-start(s32[1,256]{1,0:T(1,128)} %shared_hbm.1) | copy-start | bytes 3076
  5.2 0.7 %copy-start.4 = (s32[2]{0:T(128)S(1)}, s32[2]{0:T(128)}, u32[]{:S(2)}) copy-start(s32[2]{0:T(128)} %type_hbm.1) | copy-start | bytes 28

commit v3 on v2

v3 whole, which is shorter than its diff:
```python
import functools

import jax
import jax.numpy as jnp
from jax import lax
from jax.experimental import pallas as pl
from jax.experimental.pallas import tpu as pltpu
from jax.sharding import PartitionSpec as P

SHIFT = 0.5
INV_HALF = 0.5
GROUP = 4
WIDTHS = (128, 256)
MESH = pl.DeviceIdType.MESH
F32 = jnp.float32
BF16 = jnp.bfloat16


def dot(a, b):
    return jnp.dot(a, b, preferred_element_type=F32)


def dot_tn(a, b):
    return lax.dot_general(a, b, (((0,), (0,)), ((), ())), preferred_element_type=F32)


def dot_nt(a, b):
    return lax.dot_general(a, b, (((1,), (1,)), ((), ())), preferred_element_type=F32)


def one_hot(rows, index_row):
    spots = lax.broadcasted_iota(jnp.int32, (rows, index_row.shape[1]), 0)
    return jnp.where(spots == index_row, 1.0, 0.0).astype(BF16)


def kernel(
    doms, bands, group, chunks, inverse_count,
    type_hbm, nodes_hbm, shared_hbm, v_hbm, ham_hbm,
    filt_ref, margin_ref,
    type_ref, nodes_ref, shared_ref, v_ref, ham, hp,
    send1, ghost, send2, recv2, send3, recv3, everyone,
    part, own_part, arrived, part2, own_part2, arrived2,
    in_sem, s1, r1, s2, r2, s3, r3, s4, r4, s5, r5, s6, r6,
):
    dom = lax.axis_index("dom")
    band = lax.axis_index("band")
    nodes, cols = v_ref.shape
    cells = nodes_ref.shape[0]
    rim = shared_ref.shape[1] // 2
    slots = nodes + 2 * rim
    groups = doms // group if group else 0
    present = (dom > 0, dom < doms - 1)
    beside = (jnp.maximum(dom - 1, 0), jnp.minimum(dom + 1, doms - 1))

    load_shared, load_v, load_nodes, load_type, load_ham = [
        pltpu.make_async_copy(source, target, in_sem.at[number])
        for number, (source, target) in enumerate(
            (
                (shared_hbm, shared_ref),
                (v_hbm, v_ref),
                (nodes_hbm, nodes_ref),
                (type_hbm, type_ref),
                (ham_hbm, ham),
            )
        )
    ]

    barrier = pltpu.get_barrier_semaphore()

    def greet(other_dom, other_band):
        pl.semaphore_signal(
            barrier, inc=1,
            device_id={"dom": other_dom, "band": other_band},
            device_id_type=MESH,
        )

    if group:
        inside, stack = lax.rem(dom, group), dom // group
        mates = [stack * group + lax.rem(inside + away, group) for away in range(1, group)]
        tower = [lax.rem(stack + away, groups) * group + inside for away in range(1, groups)]
        lonely = (
            jnp.logical_and(present[0], inside == 0),
            jnp.logical_and(present[1], inside == group - 1),
        )
    else:
        mates, tower, lonely = [], [], present
    for side in (0, 1):
        @pl.when(lonely[side])
        def _():
            greet(beside[side], band)
    for mate in mates + tower:
        greet(mate, band)
    for step in range(1, bands):
        greet(dom, lax.rem(band + step, bands))
    for load in (load_shared, load_v, load_nodes, load_type, load_ham):
        load.start()

    for side in (0, 1):
        @pl.when(jnp.logical_not(present[side]))
        def _():
            ghost[side] = jnp.zeros((rim, cols), BF16)
            recv2[side] = jnp.zeros((2, rim, cols), BF16)
            recv3[side] = jnp.zeros((rim, cols), BF16)

    def swap(source, target, sent, got, chunk, side, arriving):
        low, high = chunks[chunk]
        landing = side if arriving else 1 - side
        return pltpu.make_async_remote_copy(
            src_ref=source.at[side, ..., low:high],
            dst_ref=target.at[landing, ..., low:high],
            send_sem=sent.at[chunk, side],
            recv_sem=got.at[chunk, landing],
            device_id={"dom": beside[side], "band": band},
            device_id_type=MESH,
        )

    def swap_start(*args):
        for side in (0, 1):
            @pl.when(present[side])
            def _():
                swap(*args, side, False).start()

    def swap_wait(*args):
        for side in (0, 1):
            @pl.when(present[side])
            def _():
                swap(*args, side, True).wait()

    load_shared.wait()
    load_v.wait()
    pick = one_hot(nodes, shared_ref[...])
    send1[...] = dot_tn(pick, v_ref[...]).astype(BF16).reshape(2, rim, cols)

    fixed = len(mates) + len(tower) + bands - 1
    pl.semaphore_wait(
        barrier, fixed + jnp.where(lonely[0], 1, 0) + jnp.where(lonely[1], 1, 0)
    )
    numbers = range(len(chunks))
    for chunk in numbers:
        swap_start(send1, ghost, s1, r1, chunk)

    load_nodes.wait()
    load_type.wait()
    load_ham.wait()
    for cell in range(cells):
        slot = nodes_ref[cell : cell + 1, :]
        slot = jnp.where(slot < rim, slot + nodes, jnp.where(slot < nodes + rim, slot - rim, slot))
        spread = one_hot(slots, slot)
        spread_ham = dot(spread, ham[type_ref[cell]]).astype(BF16)
        hp[cell] = dot_nt(spread_ham, spread).astype(BF16)

    def apply(low, high, own, rims):
        total = dot(hp[0, low:high, :nodes], own) + dot(hp[0, low:high, nodes:], rims)
        for cell in range(1, cells):
            total += dot(hp[cell, low:high, :nodes], own) + dot(hp[cell, low:high, nodes:], rims)
        return total

    held = []
    for chunk, (low, high) in enumerate(chunks):
        wide = high - low
        swap_wait(send1, ghost, s1, r1, chunk)
        v = v_ref[:, low:high]
        rims = ghost[:, :, low:high].reshape(2 * rim, wide)
        y_own = apply(0, nodes, v, rims)
        send2[:, 1, :, low:high] = (
            dot_tn(pick, y_own.astype(BF16)).astype(BF16).reshape(2, rim, wide)
        )
        y_rim = apply(nodes, slots, v, rims)
        send2[:, 0, :, low:high] = y_rim.astype(BF16).reshape(2, rim, wide)
        swap_start(send2, recv2, s2, r2, chunk)
        held.append((y_own, y_rim))

    again = []
    for chunk, (low, high) in enumerate(chunks):
        wide = high - low
        y_own, y_rim = held[chunk]
        v32 = v_ref[:, low:high].astype(F32)
        rims = ghost[:, :, low:high].reshape(2 * rim, wide).astype(F32)
        swap_wait(send2, recv2, s2, r2, chunk)
        y_own = y_own + dot(pick, recv2[:, 0, :, low:high].reshape(2 * rim, wide))
        y_rim = y_rim + recv2[:, 1, :, low:high].reshape(2 * rim, wide).astype(F32)
        first = ((y_own - SHIFT * v32) * INV_HALF).astype(BF16)
        first_rim = ((y_rim - SHIFT * rims) * INV_HALF).reshape(2, rim, wide)
        first_rim = jnp.concatenate(
            [jnp.where(present[side], first_rim[side], 0.0) for side in (0, 1)], axis=0
        ).astype(BF16)
        out_rim = apply(nodes, slots, first, first_rim)
        send3[:, :, low:high] = out_rim.astype(BF16).reshape(2, rim, wide)
        swap_start(send3, recv3, s3, r3, chunk)
        again.append((apply(0, nodes, first, first_rim), first))

    def share(chunk, step, arriving=False):
        low, high = chunks[chunk]
        landing = step - 1 if arriving else bands - 1 - step
        return pltpu.make_async_remote_copy(
            src_ref=filt_ref.at[:, low:high],
            dst_ref=everyone.at[landing, :, low:high],
            send_sem=s4.at[chunk, step],
            recv_sem=r4.at[chunk, landing],
            device_id={"dom": dom, "band": lax.rem(band + step, bands)},
            device_id_type=MESH,
        )

    for chunk, (low, high) in enumerate(chunks):
        wide = high - low
        second, first = again[chunk]
        v32 = v_ref[:, low:high].astype(F32)
        swap_wait(send3, recv3, s3, r3, chunk)
        second = second + dot(pick, recv3[:, :, low:high].reshape(2 * rim, wide))
        filt_ref[:, low:high] = (
            2.0 * (second - SHIFT * first.astype(F32)) * INV_HALF - v32
        ).astype(BF16)
        for step in range(1, bands):
            share(chunk, step).start()

    def give(step, away, arriving=False):
        landing = away - 1 if arriving else group - 1 - away
        target = lax.rem(inside + away, group)
        return pltpu.make_async_remote_copy(
            src_ref=part.at[step, target],
            dst_ref=arrived.at[step, landing],
            send_sem=s5.at[step, away],
            recv_sem=r5.at[step, landing],
            device_id={"dom": stack * group + target, "band": band},
            device_id_type=MESH,
        )

    def climb(step, away, arriving=False):
        landing = away - 1 if arriving else groups - 1 - away
        target = lax.rem(stack + away, groups)
        return pltpu.make_async_remote_copy(
            src_ref=part2.at[step, target],
            dst_ref=arrived2.at[step, landing],
            send_sem=s6.at[step, away],
            recv_sem=r6.at[step, landing],
            device_id={"dom": target * group + inside, "band": band},
            device_id_type=MESH,
        )

    def place(step):
        return pl.ds(pl.multiple_of(lax.rem(band + step, bands) * cols, 128), cols)

    for step in range(bands):
        if step == 0:
            other = filt_ref[...]
        else:
            for chunk in numbers:
                share(chunk, step, True).wait_recv()
            other = everyone[step - 1]
        product = dot_tn(filt_ref[...], other)
        if not group:
            margin_ref[0, :, place(step)] = product
            continue
        rows = cols // doms
        for member in range(group):
            block = jnp.concatenate(
                [
                    product[(layer * group + member) * rows : (layer * group + member + 1) * rows]
                    for layer in range(groups)
                ],
                axis=0,
            )
            own_part[step, member] = block
            part[step, member] = block.astype(BF16)
        for away in range(1, group):
            give(step, away).start()

    if group:
        for step in range(bands):
            total = own_part[step, inside]
            for away in range(1, group):
                give(step, away, True).wait_recv()
                total += arrived[step, away - 1].astype(F32)
            for layer in range(groups):
                block = total[layer * rows : (layer + 1) * rows]
                own_part2[step, layer] = block
                part2[step, layer] = block.astype(BF16)
            for away in range(1, groups):
                climb(step, away).start()
        for step in range(bands):
            total = own_part2[step, stack]
            for away in range(1, groups):
                climb(step, away, True).wait_recv()
                total += arrived2[step, away - 1].astype(F32)
            margin_ref[0, :, place(step)] = total * inverse_count
        for step in range(bands):
            for away in range(1, group):
                give(step, away).wait_send()
            for away in range(1, groups):
                climb(step, away).wait_send()
    for chunk in numbers:
        for step in range(1, bands):
            share(chunk, step).wait_send()


def solution(mesh):
    doms, bands = mesh.shape["dom"], mesh.shape["band"]

    def on_device(vectors, cell_ham, cell_type, cell_nodes, shared_nodes):
        nodes, cols = vectors.shape
        rim = shared_nodes.shape[1] // 2
        slots = nodes + 2 * rim
        rows = cols // doms
        scatter_here = cols % doms == 0 and rows % 8 == 0 and doms % GROUP == 0 and doms > GROUP
        group = GROUP if scatter_here else 0
        groups = doms // GROUP
        inverse_count = 1.0 / (nodes * doms)
        chunks = []
        for width in WIDTHS + (cols,):
            low = chunks[-1][1] if chunks else 0
            if low < cols:
                chunks.append((low, min(low + width, cols)))
        if scatter_here:
            kept = [
                pltpu.VMEM((bands, group, groups * rows, cols), BF16),
                pltpu.VMEM((bands, group, groups * rows, cols), F32),
                pltpu.VMEM((bands, group - 1, groups * rows, cols), BF16),
                pltpu.VMEM((bands, groups, rows, cols), BF16),
                pltpu.VMEM((bands, groups, rows, cols), F32),
                pltpu.VMEM((bands, groups - 1, rows, cols), BF16),
            ]
        else:
            kept = [pltpu.VMEM((8, 128), F32)] * 6
        operands = [
            pltpu.with_memory_space_constraint(operand, pltpu.HBM)
            for operand in (cell_type, cell_nodes, shared_nodes, vectors, cell_ham)
        ]
        filtered, margin = pl.pallas_call(
            functools.partial(kernel, doms, bands, group, tuple(chunks), inverse_count),
            out_shape=(
                jax.ShapeDtypeStruct((nodes, cols), BF16),
                jax.ShapeDtypeStruct((1, rows if scatter_here else cols, bands * cols), F32),
            ),
            in_specs=[pl.BlockSpec(memory_space=pltpu.HBM)] * 5,
            out_specs=(pl.BlockSpec(memory_space=pltpu.VMEM),) * 2,
            scratch_shapes=[
                pltpu.SMEM(cell_type.shape, jnp.int32),
                pltpu.VMEM(cell_nodes.shape, jnp.int32),
                pltpu.VMEM(shared_nodes.shape, jnp.int32),
                pltpu.VMEM(vectors.shape, BF16),
                pltpu.VMEM(cell_ham.shape, BF16),
                pltpu.VMEM((cell_nodes.shape[0], slots, slots), BF16),
                pltpu.VMEM((2, rim, cols), BF16),
                pltpu.VMEM((2, rim, cols), BF16),
                pltpu.VMEM((2, 2, rim, cols), BF16),
                pltpu.VMEM((2, 2, rim, cols), BF16),
                pltpu.VMEM((2, rim, cols), BF16),
                pltpu.VMEM((2, rim, cols), BF16),
                pltpu.VMEM((max(bands - 1, 1), nodes, cols), BF16),
            ]
            + kept
            + [pltpu.SemaphoreType.DMA((5,))]
            + [pltpu.SemaphoreType.DMA((len(chunks), 2))] * 6
            + [pltpu.SemaphoreType.DMA((len(chunks), bands))] * 2
            + [pltpu.SemaphoreType.DMA((bands, GROUP))] * 2
            + [pltpu.SemaphoreType.DMA((bands, groups if scatter_here else 1))] * 2,
            compiler_params=pltpu.CompilerParams(
                collective_id=0, has_side_effects=True, vmem_limit_bytes=48 << 20
            ),
        )(*operands)
        if not scatter_here:
            margin = inverse_count * lax.psum_scatter(
                margin, "dom", scatter_dimension=1, tiled=True
            )
        return filtered, margin

    in_specs = (P("dom", "band"), P(), P("dom"), P("dom", None), P("dom", None))
    out_specs = (P("dom", "band"), P("band", "dom", None))
    return jax.shard_map(
        on_device, mesh=mesh, in_specs=in_specs, out_specs=out_specs, check_vma=False
    )
```

time: 51.2 us -> 42.4 us (0.83)
  the two profiles are of different devices: /device:TPU:24 before, /device:TPU:0 now
where the time goes in v3:
time: 42.4 us; the launch traced here: 41.8 us
  Pallas kernels  39.8 us (94%)
  local copies, waits for them, and re-layouts  1.38 us (3%)
  between operations  0.64 us (2%)
    pallas_call x1, Pallas kernels, on_device(): pl.pallas_call(functools.partial(kernel, doms, bands, group, tuple(chunks...  39.8 us
    unnamed x2, local copies, waits for them, and re-layouts  1.38 us

profile of v3, /device:TPU:0, one launch (start us, length us, event | category | flops | bytes accessed | tf_op | source)
XLA Modules:
  0.0 41.8 jit_solution(4631494248890028524)
XLA Ops:
  0.6 39.8 %shard_map.68 = (bf16[512,384]{1,0:T(8,128)(2,1)S(1)}, f32[1,24,768]{2,1,0:T(8,128)S(1)}) custom-call(s32[2]{0:T(128)} %type_hbm.1, s32[2,512]{1,0:T(2,128)} %nodes_hbm.1, s32[1,256]{1,0:T(1,128)} %shared_hbm.1, bf16[512,384]{1,0:T(8,128)(2,1)} %v_hbm.1, bf16[8,512,512]{2,1,0:T(8,128)(2,1)} %ham_hbm.1), custom_call_target="tpu_custom_call" | custom-call | tf_op jit(solution)/shard_map/pallas_call | solution.py:328
  40.4 0.7 %copy.9 = bf16[512,384]{1,0:T(8,128)(2,1)} copy(bf16[512,384]{1,0:T(8,128)(2,1)S(1)} %get-tuple-element.4) | data formatting | bytes 786432
  41.2 0.6 %copy.10 = f32[1,24,768]{2,1,0:T(8,128)} copy(f32[1,24,768]{2,1,0:T(8,128)S(1)} %get-tuple-element.5) | data formatting | bytes 147456

commit v4 on v3

--- a/solution.py
+++ b/solution.py
@@ -10,7 +10,7 @@
 SHIFT = 0.5
 INV_HALF = 0.5
 GROUP = 4
-WIDTHS = (128, 256)
+WIDTHS = (128, 128, 128)
 MESH = pl.DeviceIdType.MESH
 F32 = jnp.float32
 BF16 = jnp.bfloat16

time: 42.4 us -> 41.4 us (0.976)
  Pallas kernels: 39.8 us -> 39.2 us
    pallas_call x1, Pallas kernels: 39.8 us -> 39.2 us  [on_device(): pl.pallas_call(functools.partial(kernel, doms, bands, group, tuple(chunks...]
where the time goes in v4:
time: 41.4 us; the launch traced here: 41.2 us
  Pallas kernels  39.2 us (95%)
  local copies, waits for them, and re-layouts  1.38 us (3%)
  between operations  0.64 us (2%)
    pallas_call x1, Pallas kernels, on_device(): pl.pallas_call(functools.partial(kernel, doms, bands, group, tuple(chunks...  39.2 us
    unnamed x2, local copies, waits for them, and re-layouts  1.38 us

profile of v4, /device:TPU:0, one launch (start us, length us, event | category | flops | bytes accessed | tf_op | source)
XLA Modules:
  0.0 41.2 jit_solution(4708973551538811410)
XLA Ops:
  0.6 39.2 %shard_map.68 = (bf16[512,384]{1,0:T(8,128)(2,1)S(1)}, f32[1,24,768]{2,1,0:T(8,128)S(1)}) custom-call(s32[2]{0:T(128)} %type_hbm.1, s32[2,512]{1,0:T(2,128)} %nodes_hbm.1, s32[1,256]{1,0:T(1,128)} %shared_hbm.1, bf16[512,384]{1,0:T(8,128)(2,1)} %v_hbm.1, bf16[8,512,512]{2,1,0:T(8,128)(2,1)} %ham_hbm.1), custom_call_target="tpu_custom_call" | custom-call | tf_op jit(solution)/shard_map/pallas_call | solution.py:328
  39.8 0.7 %copy.9 = bf16[512,384]{1,0:T(8,128)(2,1)} copy(bf16[512,384]{1,0:T(8,128)(2,1)S(1)} %get-tuple-element.4) | data formatting | bytes 786432
  40.6 0.6 %copy.10 = f32[1,24,768]{2,1,0:T(8,128)} copy(f32[1,24,768]{2,1,0:T(8,128)S(1)} %get-tuple-element.5) | data formatting | bytes 147456
